TPU v7x, 32 devices: a whole 2x2x4 slice. The times are simulated.
32 devices in a mesh: row: 4 (over y, x), orb: 8 (over z, core).
Axes of the slice: x: 2, y: 2, z: 4, core: 2. Of those that a mesh axis runs over, the one named last changes fastest.
Arguments:
- integrals: bfloat16 [24, 1024, 5120], P('orb', 'row'), may hold values from -6 to 6
- tile_ids: int32 [8, 40], P('row'), may hold values from 0 to 127, as said below
- coefficients: bfloat16 [1024, 16384], P('orb'), may hold values from -0.078125 to 0.078125
- metric: float32 [24, 24], replicated, may hold values from -0.0078125 to 0.0078125
Outputs:
- exchange_columns: float32 [1024, 1024], P('orb', 'row')
Inputs may be any that keep to these rules, and one draw needn't show every extreme that they name: `tile_ids`: row block b covers basis functions b * 128 to b * 128 + 127. Each row lists 40 different column tiles (tile t covers basis functions t * 128 to t * 128 + 127); the first is the block's own tile b.
All inputs are finite; a program needn't handle non-finite values.
Results may differ from a plain program's by a relative error of at most 0.022.
Values may be sent and summed in bfloat16 or wider, within the bound.
A program may use at most 128 MiB of HBM per device.

v0:
```python
import jax
import jax.numpy as jnp
from jax import lax
from jax.sharding import PartitionSpec as P


def per_device(integrals, tile_ids, coefficients, metric):
    aux_local, local_rows, kept_width = integrals.shape
    orb_local, basis_width = coefficients.shape
    block_count, kept_count = tile_ids.shape
    tile_rows = local_rows // block_count
    blocked = coefficients.reshape(orb_local, basis_width // tile_rows, tile_rows)
    picked = jnp.take(blocked, tile_ids.reshape(block_count * kept_count), axis=1)
    picked = picked.reshape(orb_local, block_count, kept_count * tile_rows)
    slabs = integrals.reshape(aux_local, block_count, tile_rows, kept_width)
    col_piece = lax.all_gather(picked, "orb", axis=0, tiled=True)
    halves = jnp.einsum("pbmk,jbk->pjbm", slabs, col_piece, preferred_element_type=jnp.float32)
    halves = halves.reshape(aux_local, col_piece.shape[0], local_rows).astype(jnp.bfloat16)
    own_piece = col_piece[:, :, :tile_rows].reshape(col_piece.shape[0], local_rows)
    stacked = jnp.concatenate([halves, own_piece[None]], axis=0)
    halves = stacked[:aux_local]
    own_rows = stacked[aux_local]
    by_orbital = lax.all_to_all(halves, "orb", split_axis=1, concat_axis=0, tiled=True)
    partial_sum = jnp.einsum(
        "qjm,im->qji", by_orbital, own_rows, preferred_element_type=jnp.float32
    )
    occupied_share = lax.psum_scatter(
        partial_sum.astype(jnp.bfloat16), "row", scatter_dimension=2, tiled=True
    ).astype(jnp.float32)
    fitted_share = jnp.einsum(
        "pq,qji->pji", metric, occupied_share, precision=lax.Precision.HIGHEST
    ).astype(jnp.bfloat16)
    fitted = lax.all_gather(fitted_share, "row", axis=2, tiled=True)
    return lax.psum_scatter(
        jnp.einsum("pjm,pji->im", by_orbital, fitted, preferred_element_type=jnp.float32).astype(
            jnp.bfloat16
        ),
        "orb",
        scatter_dimension=0,
        tiled=True,
    ).astype(jnp.float32)


def solution(mesh):
    return jax.shard_map(
        per_device,
        mesh=mesh,
        in_specs=(P("orb", "row", None), P("row", None), P("orb", None), P()),
        out_specs=P("orb", "row"),
        check_vma=False,
    )
```

profile of v0, /device:TPU:1, one launch (start us, length us, event | category | flops | bytes accessed | tf_op | source)
XLA Modules:
  0.0 479.3 jit_solution(17122439805342675751)
XLA Ops:
  6.5 0.8 reshape.51
  7.3 0.7 compare_and_fusion
  8.1 6.4 %copy.25 = bf16[128,16384]{0,1:T(8,128)(2,1)} copy(bf16[128,16384]{1,0:T(8,128)(2,1)} %param.6) | data formatting | bytes 8388608 | tf_op args[2]
  14.5 6.4 %copy.26 = bf16[128,128,128]{2,0,1:T(8,128)(2,1)} copy(bf16[128,128,128]{0,2,1:T(8,128)(2,1)} %bitcast.42) | data formatting | bytes 8388608 | tf_op jit(solution)/shard_map/reshape | solution.py:12
  20.9 3.2 gather_fusion
  24.2 2.6 copy.27
  26.7 3.0 copy.28
  29.7 1.8 broadcast_select_fusion
  31.6 188.1 %all-gather.3.cloned.1.call-done = bf16[1024,2,5120]{2,0,1:T(8,128)(2,1)} async-done(((bf16[128,2,5120]{2,0,1:T(8,128)(2,1)}), bf16[1024,2,5120]{2,0,1:T(8,128)(2,1)}) %all-gather.3.cloned.1.call-update) | async-done | bytes 20971536 | tf_op jit(solution)/shard_map/all_gather | solution.py:16
  219.7 14.0 %fusion.11 = bf16[3,1024,2,128]{1,3,0,2:T(8,128)(2,1)S(1)} fusion(bf16[3,2,128,5120]{3,2,1,0:T(8,128)(2,1)} %bitcast.51, bf16[1024,2,5120]{2,0,1:T(8,128)(2,1)} %all-gather.3.cloned.1.call-done), kind=kOutput, calls=%fused_computation.11 | convolution fusion | flops 8053850112 | bytes 30408704 | tf_op jit(solution)/shard_map/pbmk,jbk->pjbm/dot_general | solution.py:17
  233.6 0.2 copy.30
  233.8 2.6 copy.31
  236.4 3.9 all-to-all-start
  240.3 0.2 copy.34
  240.5 47.9 %all-to-all-done = bf16[3,1024,256]{2,0,1:T(4,128)(2,1)S(1)} async-done(((bf16[3,1024,256]{2,0,1:T(4,128)(2,1)}), bf16[3,1024,256]{2,0,1:T(4,128)(2,1)S(1)}, u32[]{:S(2)}, u32[]{:S(2)}) %all-to-all-start) | async-done | bytes 1572896 | tf_op jit(solution)/shard_map/all_to_all | solution.py:23
  288.4 0.2 copy.32
  288.6 0.1 copy.33
  288.7 4.5 convolution_convert_fusion
  293.3 69.1 %reduce-scatter.3.cloned.1.call-done = bf16[24,128,256]{2,1,0:T(8,128)(2,1)} async-done(((bf16[24,128,1024]{2,1,0:T(8,128)(2,1)}), bf16[24,128,256]{2,1,0:T(8,128)(2,1)}) %reduce-scatter.3.cloned.1.call-update) | async-done | bytes 1572880 | tf_op jit(solution)/shard_map/reduce_scatter | solution.py:27
  362.3 4.5 fusion.16
  366.9 70.0 %all-gather.5.cloned.1.call-done = bf16[24,128,1024]{2,0,1:T(8,128)(2,1)} async-done(((bf16[24,128,256]{2,0,1:T(8,128)(2,1)}), bf16[24,128,1024]{2,0,1:T(8,128)(2,1)}) %all-gather.5.cloned.1.call-update) | async-done | bytes 6291472 | tf_op jit(solution)/shard_map/all_gather | solution.py:33
  436.9 6.0 %fusion.22 = bf16[1024,256]{1,0:T(8,128)(2,1)} fusion(bf16[24,128,1024]{2,0,1:T(8,128)(2,1)} %all-gather.5.cloned.1.call-done, bf16[24,128,256]{2,1,0:T(8,128)(2,1)S(1)} %bitcast.46), kind=kOutput, calls=%fused_computation.14 | convolution fusion | flops 1610874880 | bytes 8388608 | tf_op jit(solution)/shard_map/pjm,pji->im/dot_general | solution.py:35
  443.0 28.3 %reduce-scatter.5.cloned.1.call-done = bf16[128,256]{1,0:T(8,128)(2,1)} async-done(((bf16[1024,256]{1,0:T(8,128)(2,1)}), bf16[128,256]{1,0:T(8,128)(2,1)}) %reduce-scatter.5.cloned.1.call-update) | async-done | bytes 65552 | tf_op jit(solution)/shard_map/reduce_scatter | solution.py:34
  471.3 1.5 convert_element_type.32
  (16 shorter events, 0.3 us)
Async XLA Ops:
  6.5 355.8 %copy-start = (f32[24,24]{1,0:T(8,128)S(1)}, f32[24,24]{1,0:T(8,128)}, u32[]{:S(2)}) copy-start(f32[24,24]{1,0:T(8,128)} %param.7) | copy-start | bytes 6916
  6.5 213.1 %all-gather.3.cloned.1.call-start = ((), (), s32[]{:S(2)}) async-start(), calls=%async_computation.3 | async-start | bytes 23592960 | tf_op jit(solution)/shard_map/all_gather | solution.py:16
  236.4 3.9 slice-start
  236.4 52.0 %all-to-all-start = ((bf16[3,1024,256]{2,0,1:T(4,128)(2,1)}), bf16[3,1024,256]{2,0,1:T(4,128)(2,1)S(1)}, u32[]{:S(2)}, u32[]{:S(2)}) async-start(bf16[3,1024,256]{2,0,1:T(4,128)(2,1)} %copy.31), calls=%async_computation | async-start | bytes 4194304 | tf_op jit(solution)/shard_map/all_to_all | solution.py:23
  240.3 122.0 %reduce-scatter.3.cloned.1.call-start = ((), (), s32[]{:S(2)}) async-start(), calls=%async_computation.4 | async-start | bytes 7864320 | tf_op jit(solution)/shard_map/reduce_scatter | solution.py:27
  293.2 143.7 %all-gather.5.cloned.1.call-start = ((), (), s32[]{:S(2)}) async-start(), calls=%async_computation.5 | async-start | bytes 7864320 | tf_op jit(solution)/shard_map/all_gather | solution.py:33
  366.9 104.4 %reduce-scatter.5.cloned.1.call-start = ((), (), s32[]{:S(2)}) async-start(), calls=%async_computation.6 | async-start | bytes 589824 | tf_op jit(solution)/shard_map/reduce_scatter | solution.py:34
Sparse Core Ops, SparseCore 0:
  31.7 187.9 all-gather.2
  293.3 68.9 reduce-scatter.2
  367.0 69.9 all-gather.4
  443.1 28.1 reduce-scatter.4
where the time goes:
time: 484 us; the launch traced here: 479 us
  waiting for transfers between devices  403 us (83%)
  matrix products  28.9 us (6%)
  local copies, waits for them, and re-layouts  25.8 us (5%)
  between operations  13.2 us (3%)
    all_gather x1, waiting for transfers between devices, per_device(): col_piece = lax.all_gather(picked, 'orb', axis=0, tiled=True)  188 us
    all_gather x1, waiting for transfers between devices, per_device(): fitted = lax.all_gather(fitted_share, 'row', axis=2, tiled=True)  70 us
    reduce_scatter x1, waiting for transfers between devices, per_device(): lax.psum_scatter(partial_sum.astype(jnp.bfloat16), 'row', scatter_dimensi...  69.1 us
    all_to_all x1, waiting for transfers between devices, per_device(): lax.all_to_all(halves, 'orb', split_axis=1, concat_axis=0, tiled=True)  47.9 us
    reduce_scatter x1, waiting for transfers between devices, per_device(): lax.psum_scatter(jnp.einsum('pjm,pji->im', by_orbital, fitted, preferred_...  28.3 us
    dot_general x1, matrix products, per_device(): jnp.einsum('pbmk,jbk->pjbm', slabs, col_piece, preferred_element_type=jnp...  14 us
  transfers between devices with their start and end apart: 5, of which 5 were waited for; matrix products, arithmetic and copies ran while one was open for 0% of the time, Pallas kernels for 0%

commit v1 on v0

v1 whole, which is shorter than its diff:
```python
import functools

import jax
import jax.numpy as jnp
from jax import lax
from jax.experimental import pallas as pl
from jax.experimental.pallas import tpu as pltpu
from jax.sharding import PartitionSpec as P


def pick_kernel(count, tile, ids_ref, coef_ref, out_ref, sem):
    def begin(slot, carry):
        source = pl.ds(pl.multiple_of(ids_ref[slot] * tile, tile), tile)
        target = pl.ds(pl.multiple_of(slot * tile, tile), tile)
        pltpu.make_async_copy(coef_ref.at[:, source], out_ref.at[:, target], sem).start()
        return carry

    lax.fori_loop(0, count, begin, 0)
    pltpu.make_async_copy(coef_ref.at[:, pl.ds(0, count * tile)], out_ref, sem).wait()


def pick(coefficients, ids, tile):
    count = ids.shape[0]
    return pl.pallas_call(
        functools.partial(pick_kernel, count, tile),
        out_shape=jax.ShapeDtypeStruct((coefficients.shape[0], count * tile), coefficients.dtype),
        in_specs=[
            pl.BlockSpec(memory_space=pltpu.SMEM),
            pl.BlockSpec(memory_space=pl.ANY),
        ],
        out_specs=pl.BlockSpec(memory_space=pltpu.VMEM),
        scratch_shapes=[pltpu.SemaphoreType.DMA],
    )(ids, coefficients)


def per_device(rows, orbs, integrals, tile_ids, coefficients, metric):
    aux_local, local_rows, kept_width = integrals.shape
    orb_local, basis_width = coefficients.shape
    block_count, kept_count = tile_ids.shape
    tile_rows = local_rows // block_count
    orbitals = orb_local * orbs
    aux = aux_local * orbs
    window = local_rows * rows
    part = orbitals // (rows * orbs)
    picked = pick(coefficients, tile_ids.reshape(block_count * kept_count), tile_rows)
    col_piece = lax.all_gather(picked, "orb", axis=0, tiled=True)
    slabs = integrals.reshape(aux_local, block_count, tile_rows, kept_width)
    halves = [
        jnp.einsum(
            "pmk,jk->pjm",
            slabs[:, b],
            col_piece[:, b * kept_width : (b + 1) * kept_width],
            preferred_element_type=jnp.float32,
        ).astype(jnp.bfloat16)
        for b in range(block_count)
    ]
    halves = jnp.concatenate(halves, axis=2)
    outgoing = halves.reshape(aux_local, rows * orbs, part, local_rows).transpose(1, 0, 2, 3)
    by_part = lax.all_to_all(outgoing, ("row", "orb"), split_axis=0, concat_axis=0, tiled=True)
    by_part = by_part.reshape(rows, aux, part, local_rows)
    mixed = jnp.einsum(
        "pq,rpjm->rqjm", metric, by_part.astype(jnp.float32), precision=lax.Precision.HIGHEST
    ).astype(jnp.bfloat16)
    gram = jnp.einsum(
        "rqjm,sqjn->rmsn", by_part, mixed, preferred_element_type=jnp.float32
    ).astype(jnp.bfloat16)
    gram = gram.reshape(orbs, window // orbs, rows, local_rows).transpose(2, 0, 1, 3)
    gram = gram.reshape(rows * window, local_rows)
    share = lax.psum_scatter(gram, ("row", "orb"), scatter_dimension=0, tiled=True)
    columns = lax.all_gather(share, "orb", axis=0, tiled=True)
    return jnp.dot(coefficients[:, :window], columns, preferred_element_type=jnp.float32)


def solution(mesh):
    return jax.shard_map(
        functools.partial(per_device, mesh.shape["row"], mesh.shape["orb"]),
        mesh=mesh,
        in_specs=(P("orb", "row", None), P("row", None), P("orb", None), P()),
        out_specs=P("orb", "row"),
        check_vma=False,
    )
```

time: 484 us -> 427 us (0.88)
  waiting for transfers between devices: 403 us -> 319 us
  blocking collectives: 0 us -> 61.4 us
  local copies, waits for them, and re-layouts: 25.8 us -> 4.33 us
  matrix products: 28.9 us -> 23.7 us
    all_gather x1 -> x0, waiting for transfers between devices: 70 us -> none  [per_device(): fitted = lax.all_gather(fitted_share, 'row', axis=2, tiled=True)]
    all_to_all x1 -> x0, waiting for transfers between devices: 47.9 us -> none  [per_device(): lax.all_to_all(halves, 'orb', split_axis=1, concat_axis=0, tiled=True)]
    all_to_all x0 -> x1, blocking collectives: none -> 41.2 us  [per_device(): lax.all_to_all(outgoing, ('row', 'orb'), split_axis=0, concat_axis=0, til...]
    reduce_scatter x2 -> x1, waiting for transfers between devices: 97.4 us -> 131 us  [per_device(): lax.psum_scatter(gram, ('row', 'orb'), scatter_dimension=0, tiled=True)]
    all_gather x0 -> x1, blocking collectives: none -> 20.3 us  [per_device(): columns = lax.all_gather(share, 'orb', axis=0, tiled=True)]
    gather x3 -> x0, local copies, waits for them, and re-layouts: 8.8 us -> none  [per_device(): jnp.take(blocked, tile_ids.reshape(block_count * kept_count), axis=1)]
    unnamed x5 -> x2, local copies, waits for them, and re-layouts: 6.48 us -> 0.01 us
    reshape x1 -> x0, local copies, waits for them, and re-layouts: 6.42 us -> none  [per_device(): coefficients.reshape(orb_local, basis_width // tile_rows, tile_rows)]
  transfers between devices with their start and end apart: 5 -> 2, of which waited for: 5 -> 2; matrix products, arithmetic and copies ran while one was open for 0% -> 0% of each run, Pallas kernels for 0% -> 0%
where the time goes in v1:
time: 427 us
  waiting for transfers between devices  319 us (75%)
  blocking collectives  61.4 us (14%)
  matrix products  23.7 us (6%)
  between operations  13.5 us (3%)
  local copies, waits for them, and re-layouts  4.33 us (1%)
    all_gather x1, waiting for transfers between devices, per_device(): col_piece = lax.all_gather(picked, 'orb', axis=0, tiled=True)  188 us
    reduce_scatter x1, waiting for transfers between devices, per_device(): lax.psum_scatter(gram, ('row', 'orb'), scatter_dimension=0, tiled=True)  131 us
    all_to_all x1, blocking collectives, per_device(): lax.all_to_all(outgoing, ('row', 'orb'), split_axis=0, concat_axis=0, til...  41.2 us
    all_gather x1, blocking collectives, per_device(): columns = lax.all_gather(share, 'orb', axis=0, tiled=True)  20.3 us
    dot_general x2, matrix products, per_device(): jnp.einsum('pmk,jk->pjm', slabs[:, b], col_piece[:, b * kept_width:(b + 1...  18.7 us
  transfers between devices with their start and end apart: 2, of which 2 were waited for; matrix products, arithmetic and copies ran while one was open for 0% of the time, Pallas kernels for 0%

profile of v1, /device:TPU:1, one launch (start us, length us, event | category | flops | bytes accessed | tf_op | source)
XLA Modules:
  0.0 426.5 jit_solution(15319204729082173327)
XLA Ops:
  6.5 0.0 copy-start
  6.5 0.0 all-gather.2.cloned.1.call-start
  6.5 1.3 reshape.18.ids_ref
  7.8 4.0 shard_map.46
  11.9 0.0 all-gather.2.cloned.1.call-update
  11.9 0.0 reduce-scatter.2.cloned.1.call-start
  11.9 188.0 %all-gather.2.cloned.1.call-done = bf16[1024,10240]{1,0:T(8,128)(2,1)} async-done(((bf16[128,10240]{1,0:T(8,128)(2,1)}), bf16[1024,10240]{1,0:T(8,128)(2,1)}) %all-gather.2.cloned.1.call-update) | async-done | bytes 20971536 | tf_op jit(solution)/shard_map/all_gather | solution.py:46
  200.0 9.3 %fusion.9 = bf16[3,1024,128]{1,2,0:T(8,128)(2,1)S(1)} fusion(bf16[3,2,128,5120]{3,2,1,0:T(8,128)(2,1)} %bitcast.68, bf16[1024,10240]{1,0:T(8,128)(2,1)} %all-gather.2.cloned.1.call-done), kind=kOutput, calls=%fused_computation.14 | convolution fusion | flops 4026925056 | bytes 15204352 | tf_op jit(solution)/shard_map/pmk,jk->pjm/dot_general | solution.py:49
  209.3 9.3 %fusion.10 = bf16[3,1024,128]{1,2,0:T(8,128)(2,1)S(1)} fusion(bf16[3,2,128,5120]{3,2,1,0:T(8,128)(2,1)} %bitcast.69, bf16[1024,10240]{1,0:T(8,128)(2,1)} %all-gather.2.cloned.1.call-done), kind=kOutput, calls=%fused_computation.15 | convolution fusion | flops 4026925056 | bytes 15204352 | tf_op jit(solution)/shard_map/pmk,jk->pjm/dot_general | solution.py:49
  218.7 0.1 pad_maximum_fusion
  218.8 0.7 copy.24
  219.5 0.1 copy.25
  219.6 41.2 %all_to_all.5 = bf16[32,3,32,256]{3,2,1,0:T(8,128)(2,1)S(1)} all-to-all(bf16[32,3,32,256]{3,2,1,0:T(8,128)(2,1)S(1)} %copy.25), channel_id=1, replica_groups=mesh['row'=4,'orb'=8] {'row','orb'}, dimensions={0} | all-to-all | bytes 3145728 | tf_op jit(solution)/shard_map/all_to_all | solution.py:59
  260.8 0.0 copy-done
  260.8 1.9 fusion.4
  262.7 1.8 bitcast_convert_fusion
  264.6 1.5 copy.29
  266.0 0.0 reduce-scatter.2.cloned.1.call-update
  266.0 131.3 %reduce-scatter.2.cloned.1.call-done = bf16[128,256]{1,0:T(8,128)(2,1)} async-done(((bf16[4096,256]{1,0:T(8,128)(2,1)}), bf16[128,256]{1,0:T(8,128)(2,1)}) %reduce-scatter.2.cloned.1.call-update) | async-done | bytes 65552 | tf_op jit(solution)/shard_map/reduce_scatter | solution.py:69
  397.4 20.3 %all_gather.7 = bf16[1024,256]{1,0:T(8,128)(2,1)S(1)} all-gather(bf16[128,256]{1,0:T(8,128)(2,1)} %reduce-scatter.2.cloned.1.call-done), channel_id=1, replica_groups=mesh['row'=4,'orb'=8] {'orb'}, dimensions={0}, use_global_device_ids=true | all-gather | bytes 589824 | tf_op jit(solution)/shard_map/all_gather | solution.py:70
  417.7 1.3 convolution_bitcast_fusion
  418.9 0.8 copy.30
Async XLA Ops:
  6.5 254.3 %copy-start = (f32[24,24]{1,0:T(8,128)S(1)}, f32[24,24]{1,0:T(8,128)}, u32[]{:S(2)}) copy-start(f32[24,24]{1,0:T(8,128)} %param.7) | copy-start | bytes 6916
  6.5 193.4 %all-gather.2.cloned.1.call-start = ((), (), s32[]{:S(2)}) async-start(), calls=%async_computation.2 | async-start | bytes 23592960 | tf_op jit(solution)/shard_map/all_gather | solution.py:46
  11.9 385.5 %reduce-scatter.2.cloned.1.call-start = ((), (), s32[]{:S(2)}) async-start(), calls=%async_computation.3 | async-start | bytes 2162688 | tf_op jit(solution)/shard_map/reduce_scatter | solution.py:69
Sparse Core Ops, SparseCore 0:
  12.0 187.9 all-gather.1
  266.2 131.1 reduce-scatter.1

commit v2 on v1

--- a/solution.py
+++ b/solution.py
@@ -33,7 +33,388 @@
     )(ids, coefficients)
 
 
+MESH = pl.DeviceIdType.MESH
+CORES = 2
+SPLIT = 2
+
+
+def greet(peers):
+    barrier = pltpu.get_barrier_semaphore()
+    for peer in peers:
+        pl.semaphore_signal(barrier, inc=1, device_id=peer, device_id_type=MESH)
+    pl.semaphore_wait(barrier, len(peers))
+
+
+def remote(source, target, send, recv, device):
+    return pltpu.make_async_remote_copy(
+        src_ref=source,
+        dst_ref=target,
+        send_sem=send,
+        recv_sem=recv,
+        device_id=device,
+        device_id_type=MESH,
+    )
+
+
+def gather_kernel(dims, ids_ref, coef_ref, ints_ref, kept_ref, other_ref, *scratch):
+    rows, chips, orb_local, tile, count = dims
+    quarter = orb_local // rows
+    piece = quarter // SPLIT
+    routes = [(d, s) for d in range(1, chips) for s in (1, -1)]
+    scratch = list(scratch)
+    raw = {}
+    for route in range(len(routes)):
+        for h in range(SPLIT):
+            raw[route, h] = scratch.pop(0)
+    staged = {}
+    for route in range(len(routes)):
+        for h in range(SPLIT):
+            for t in range(rows):
+                staged[route, h, t] = scratch.pop(0)
+    own, own_kept, ids_v, ids_s, z_send, z_recv, p_send, p_recv, l_sem, i_send, i_recv = scratch
+    row = lax.axis_index("row")
+    orb = lax.axis_index("orb")
+    chip = orb // CORES
+    core = orb % CORES
+    row_peers = [(lax.rem(row + t, rows), orb) for t in range(1, rows)]
+    chip_peers = [(row, lax.rem(chip + d, chips) * CORES + core) for d in range(1, chips)]
+    partner = (row, chip * CORES + 1 - core)
+    greet(row_peers + chip_peers + [partner])
+
+    def z_copy(route, h, device):
+        rows_at = pl.ds(pl.multiple_of(row * quarter + h * piece, piece), piece)
+        return remote(
+            own.at[:, rows_at, :],
+            raw[route, h],
+            z_send.at[route, h],
+            z_recv.at[route, h],
+            device,
+        )
+
+    def towards(route):
+        d, s = routes[route]
+        there = chip + s * d
+        return there, (there >= 0) & (there < chips)
+
+    def origin(route):
+        d, s = routes[route]
+        there = chip - s * d
+        return there, (there >= 0) & (there < chips)
+
+    tiles = own.shape[0]
+
+    def fetch(index, carry):
+        at = pl.ds(pl.multiple_of(index * tile, tile), tile)
+        pltpu.make_async_copy(coef_ref.at[:, at], own.at[index], l_sem.at[0]).start()
+        return carry
+
+    lax.fori_loop(0, tiles, fetch, 0)
+    id_copies = []
+    for t in range(1, rows):
+        id_copies.append(
+            remote(ids_ref, ids_v.at[t], i_send.at[t], i_recv.at[t], row_peers[t - 1])
+        )
+        id_copies[-1].start()
+
+    def landed(index, carry):
+        at = pl.ds(pl.multiple_of(index * tile, tile), tile)
+        pltpu.make_async_copy(coef_ref.at[:, at], own.at[index], l_sem.at[0]).wait()
+        return carry
+
+    lax.fori_loop(0, tiles, landed, 0)
+    for route in range(len(routes)):
+        there, valid = towards(route)
+        for h in range(SPLIT):
+
+            @pl.when(valid)
+            def _():
+                z_copy(route, h, (row, there * CORES + core)).start()
+
+    swap = remote(ints_ref, other_ref, i_send.at[0], i_recv.at[0], partner)
+    swap.start()
+    first = pltpu.make_async_copy(ids_ref, ids_s.at[0], l_sem.at[1])
+    first.start()
+    first.wait()
+    for t in range(1, rows):
+        id_copies[t - 1].wait()
+        move = pltpu.make_async_copy(ids_v.at[t], ids_s.at[t], l_sem.at[1])
+        move.start()
+        move.wait()
+
+    def take(source, target, t):
+        step = 8
+
+        def some(block, carry):
+            for k in range(step):
+                slot = block * step + k
+                at = pl.multiple_of(slot * tile, tile)
+                target[:, pl.ds(at, tile)] = source[ids_s[t, 0, slot]]
+            return carry
+
+        lax.fori_loop(0, count // step, some, 0)
+
+    take(own, own_kept, 0)
+    own_rows = pl.ds(pl.multiple_of(chip * orb_local, orb_local), orb_local)
+    keep_own = pltpu.make_async_copy(own_kept, kept_ref.at[own_rows, :], l_sem.at[0])
+    keep_own.start()
+
+    def spread(route, h, t, from_row, from_chip, device):
+        start = pl.multiple_of(from_chip * orb_local + from_row * quarter + h * piece, piece)
+        return remote(
+            staged[route, h, t],
+            kept_ref.at[pl.ds(start, piece), :],
+            p_send.at[route, h, t],
+            p_recv.at[route, h, t],
+            device,
+        )
+
+    def local(route, h, from_chip):
+        start = pl.multiple_of(from_chip * orb_local + row * quarter + h * piece, piece)
+        return pltpu.make_async_copy(
+            staged[route, h, 0], kept_ref.at[pl.ds(start, piece), :], p_send.at[route, h, 0]
+        )
+
+    for d in range(1, chips):
+        for h in range(SPLIT):
+            for route in range(len(routes)):
+                if routes[route][0] != d:
+                    continue
+                came, valid = origin(route)
+
+                @pl.when(valid)
+                def _():
+                    z_copy(route, h, partner).wait_recv()
+                    for t in range(1, rows):
+                        take(raw[route, h], staged[route, h, t], t)
+                        spread(route, h, t, row, came, row_peers[rows - t - 1]).start()
+                    take(raw[route, h], staged[route, h, 0], 0)
+                    local(route, h, came).start()
+
+    for route in range(len(routes)):
+        there, sent = towards(route)
+        came, valid = origin(route)
+        for h in range(SPLIT):
+
+            @pl.when(sent)
+            def _():
+                z_copy(route, h, (row, there * CORES + core)).wait_send()
+
+            @pl.when(valid)
+            def _():
+                local(route, h, came).wait()
+                for t in range(1, rows):
+                    spread(route, h, t, row, came, row_peers[rows - t - 1]).wait_send()
+                    source_row = lax.rem(row + t, rows)
+                    spread(route, h, t, source_row, came, row_peers[0]).wait_recv()
+
+    keep_own.wait()
+    swap.wait()
+
+
+def gather(integrals, ids, coefficients, rows, orbs, tile, count):
+    chips = orbs // CORES
+    orb_local, basis = coefficients.shape
+    piece = orb_local // rows // SPLIT
+    routes = 2 * (chips - 1)
+    dtype = coefficients.dtype
+    scratch = [pltpu.VMEM((basis // tile, piece, tile), dtype) for _ in range(routes * SPLIT)]
+    scratch += [pltpu.VMEM((piece, count * tile), dtype) for _ in range(routes * SPLIT * rows)]
+    scratch += [
+        pltpu.VMEM((basis // tile, orb_local, tile), dtype),
+        pltpu.VMEM((orb_local, count * tile), dtype),
+        pltpu.VMEM((rows, 1, ids.shape[1]), jnp.int32),
+        pltpu.SMEM((rows, 1, ids.shape[1]), jnp.int32),
+        pltpu.SemaphoreType.DMA((routes, SPLIT)),
+        pltpu.SemaphoreType.DMA((routes, SPLIT)),
+        pltpu.SemaphoreType.DMA((routes, SPLIT, rows)),
+        pltpu.SemaphoreType.DMA((routes, SPLIT, rows)),
+        pltpu.SemaphoreType.DMA((2,)),
+        pltpu.SemaphoreType.DMA((rows,)),
+        pltpu.SemaphoreType.DMA((rows,)),
+    ]
+    return pl.pallas_call(
+        functools.partial(gather_kernel, (rows, chips, orb_local, tile, count)),
+        out_shape=(
+            jax.ShapeDtypeStruct((chips * orb_local, count * tile), dtype),
+            jax.ShapeDtypeStruct(integrals.shape, integrals.dtype),
+        ),
+        in_specs=[pl.BlockSpec(memory_space=pltpu.VMEM)]
+        + [pl.BlockSpec(memory_space=pl.ANY)] * 2,
+        out_specs=(pl.BlockSpec(memory_space=pl.ANY), pl.BlockSpec(memory_space=pl.ANY)),
+        scratch_shapes=scratch,
+        compiler_params=pltpu.CompilerParams(
+            collective_id=0, has_side_effects=True, vmem_limit_bytes=56 << 20
+        ),
+    )(ids, coefficients, integrals)
+
+
+def exchange_kernel(rows, chips, in_ref, out_ref, send, recv, l_sem):
+    row = lax.axis_index("row")
+    orb = lax.axis_index("orb")
+    core = orb % CORES
+    me = row * chips + orb // CORES
+    total = rows * chips
+
+    def place(k):
+        other = lax.rem(me + k, total)
+        return other, (other // chips, lax.rem(other, chips) * CORES + core)
+
+    greet([place(k)[1] for k in range(1, total)])
+    stay = pltpu.make_async_copy(in_ref.at[me], out_ref.at[me], l_sem)
+    stay.start()
+    copies = []
+    for k in range(1, total):
+        other, device = place(k)
+        copies.append(
+            remote(in_ref.at[other], out_ref.at[me], send.at[k], recv.at[k], device)
+        )
+        copies[-1].start()
+    stay.wait()
+    for k in range(1, total):
+        copies[k - 1].wait_send()
+        other, device = place(total - k)
+        remote(in_ref.at[me], out_ref.at[other], send.at[k], recv.at[k], device).wait_recv()
+
+
+def exchange(outgoing, rows, chips):
+    total = rows * chips
+    return pl.pallas_call(
+        functools.partial(exchange_kernel, rows, chips),
+        out_shape=jax.ShapeDtypeStruct(outgoing.shape, outgoing.dtype),
+        in_specs=[pl.BlockSpec(memory_space=pltpu.VMEM)],
+        out_specs=pl.BlockSpec(memory_space=pltpu.VMEM),
+        scratch_shapes=[
+            pltpu.SemaphoreType.DMA((total,)),
+            pltpu.SemaphoreType.DMA((total,)),
+            pltpu.SemaphoreType.DMA,
+        ],
+        compiler_params=pltpu.CompilerParams(collective_id=1, has_side_effects=True),
+    )(outgoing)
+
+
+def finish_kernel(rows, orbs, gram_ref, coef_ref, out_ref, *scratch):
+    (part1, sum1, part2, share, full, send1, recv1, send2, recv2, send3, recv3) = scratch
+    row = lax.axis_index("row")
+    orb = lax.axis_index("orb")
+    height = share.shape[0]
+    row_peers = [lax.rem(row + t, rows) for t in range(1, rows)]
+    orb_peers = [lax.rem(orb + t, orbs) for t in range(1, orbs)]
+    greet([(peer, orb) for peer in row_peers] + [(row, peer) for peer in orb_peers])
+    copies = []
+    for t, peer in enumerate(row_peers):
+        copies.append(
+            remote(gram_ref.at[peer], part1.at[t], send1.at[t], recv1.at[t], (peer, orb))
+        )
+        copies[-1].start()
+    for copy in copies:
+        copy.wait()
+    total = gram_ref[row].astype(jnp.float32)
+    for t in range(rows - 1):
+        total = total + part1[t].astype(jnp.float32)
+    sum1[...] = total.astype(sum1.dtype).reshape(sum1.shape)
+    copies = []
+    for t, peer in enumerate(orb_peers):
+        copies.append(
+            remote(sum1.at[peer], part2.at[t], send2.at[t], recv2.at[t], (row, peer))
+        )
+        copies[-1].start()
+    for copy in copies:
+        copy.wait()
+    total = sum1[orb].astype(jnp.float32)
+    for t in range(orbs - 1):
+        total = total + part2[t].astype(jnp.float32)
+    share[...] = total.astype(share.dtype)
+    own_rows = pl.ds(pl.multiple_of(orb * height, height), height)
+    copies = []
+    for t, peer in enumerate(orb_peers):
+        copies.append(
+            remote(share, full.at[own_rows, :], send3.at[t], recv3.at[t], (row, peer))
+        )
+        copies[-1].start()
+    full[own_rows, :] = share[...]
+    for t in range(orbs - 1):
+        copies[t].wait_send()
+        source = lax.rem(orb + orbs - t - 1, orbs)
+        rows_at = pl.ds(pl.multiple_of(source * height, height), height)
+        remote(
+            share, full.at[rows_at, :], send3.at[t], recv3.at[t], (row, orb_peers[0])
+        ).wait_recv()
+    out_ref[...] = jnp.dot(coef_ref[...], full[...], preferred_element_type=jnp.float32)
+
+
+def finish(gram, coefs, rows, orbs):
+    _, window, width = gram.shape
+    height = window // orbs
+    dtype = gram.dtype
+    return pl.pallas_call(
+        functools.partial(finish_kernel, rows, orbs),
+        out_shape=jax.ShapeDtypeStruct((coefs.shape[0], width), jnp.float32),
+        in_specs=[pl.BlockSpec(memory_space=pltpu.VMEM)] * 2,
+        out_specs=pl.BlockSpec(memory_space=pltpu.VMEM),
+        scratch_shapes=[
+            pltpu.VMEM((rows - 1, window, width), dtype),
+            pltpu.VMEM((orbs, height, width), dtype),
+            pltpu.VMEM((orbs - 1, height, width), dtype),
+            pltpu.VMEM((height, width), dtype),
+            pltpu.VMEM((window, width), dtype),
+            pltpu.SemaphoreType.DMA((rows,)),
+            pltpu.SemaphoreType.DMA((rows,)),
+            pltpu.SemaphoreType.DMA((orbs,)),
+            pltpu.SemaphoreType.DMA((orbs,)),
+            pltpu.SemaphoreType.DMA((orbs,)),
+            pltpu.SemaphoreType.DMA((orbs,)),
+        ],
+        compiler_params=pltpu.CompilerParams(collective_id=2, has_side_effects=True),
+    )(gram, coefs)
+
+
 def per_device(rows, orbs, integrals, tile_ids, coefficients, metric):
+    aux_local, local_rows, kept_width = integrals.shape
+    orb_local, basis_width = coefficients.shape
+    block_count, kept_count = tile_ids.shape
+    if orb_local % (16 * SPLIT * rows) or orbs % CORES or (block_count * kept_count) % 8:
+        return plain_device(rows, orbs, integrals, tile_ids, coefficients, metric)
+    tile_rows = local_rows // block_count
+    chips = orbs // CORES
+    aux = aux_local * orbs
+    window = local_rows * rows
+    count = block_count * kept_count
+    held = chips * orb_local
+    part = held // (rows * chips)
+    lanes = -(-count // 128) * 128
+    ids = jnp.pad(tile_ids.reshape(1, count), ((0, 0), (0, lanes - count)))
+    kept, other = gather(integrals, ids, coefficients, rows, orbs, tile_rows, count)
+    halves = []
+    for source in (integrals, other):
+        slabs = source.reshape(aux_local, block_count, tile_rows, kept_width)
+        blocks = [
+            jnp.einsum(
+                "pmk,jk->pjm",
+                slabs[:, b],
+                kept[:, b * kept_width : (b + 1) * kept_width],
+                preferred_element_type=jnp.float32,
+            ).astype(jnp.bfloat16)
+            for b in range(block_count)
+        ]
+        halves.append(jnp.concatenate(blocks, axis=2))
+    halves = jnp.concatenate(halves, axis=0)
+    outgoing = halves.reshape(CORES * aux_local, rows * chips, part, local_rows)
+    by_part = exchange(outgoing.transpose(1, 0, 2, 3), rows, chips)
+    by_part = by_part.reshape(rows, aux, part, local_rows)
+    core = lax.axis_index("orb") % CORES
+    order = metric.reshape(chips, CORES, aux_local, chips, CORES, aux_local)
+    order = jnp.where(core == 0, order, order[:, ::-1, :, :, ::-1, :]).reshape(aux, aux)
+    mixed = jnp.einsum(
+        "pq,rpjm->rqjm", order, by_part.astype(jnp.float32), precision=lax.Precision.HIGHEST
+    ).astype(jnp.bfloat16)
+    gram = jnp.einsum(
+        "rqjm,sqjn->srmn", by_part, mixed, preferred_element_type=jnp.float32
+    ).astype(jnp.bfloat16)
+    gram = gram.reshape(rows, window, local_rows)
+    return finish(gram, coefficients[:, :window], rows, orbs)
+
+
+def plain_device(rows, orbs, integrals, tile_ids, coefficients, metric):
     aux_local, local_rows, kept_width = integrals.shape
     orb_local, basis_width = coefficients.shape
     block_count, kept_count = tile_ids.shape

time: 427 us -> 273 us (0.64)
  waiting for transfers between devices: 319 us -> 0 us
  Pallas kernels: 4.03 us -> 240 us
  blocking collectives: 61.4 us -> 0 us
  between operations: 13.5 us -> 0.17 us
  local copies, waits for them, and re-layouts: 4.33 us -> 10.3 us
    pallas_call x1 -> x3, Pallas kernels: 4.03 us -> 240 us  [the longest x1 145 us: gather(): pl.pallas_call(functools.partial(gather_kernel, (rows, chips, orb_local,...]
    all_gather x1 -> x0, waiting for transfers between devices: 188 us -> none  [per_device(): col_piece = lax.all_gather(picked, 'orb', axis=0, tiled=True)]
    reduce_scatter x1 -> x0, waiting for transfers between devices: 131 us -> none  [per_device(): lax.psum_scatter(gram, ('row', 'orb'), scatter_dimension=0, tiled=True)]
    all_to_all x1 -> x0, blocking collectives: 41.2 us -> none  [per_device(): lax.all_to_all(outgoing, ('row', 'orb'), split_axis=0, concat_axis=0, til...]
    all_gather x1 -> x0, blocking collectives: 20.3 us -> none  [per_device(): columns = lax.all_gather(share, 'orb', axis=0, tiled=True)]
    unnamed x2 -> x11, local copies, waits for them, and re-layouts: 0.01 us -> 4.64 us
    dot_general x5 -> x6, matrix products: 23.7 us -> 20.6 us  [the longest x4 12.7 us: per_device(): jnp.einsum('pmk,jk->pjm', slabs[:, b], kept[:, b * kept_width:(b + 1) * k...]
  transfers between devices with their start and end apart: 2 -> 0, of which waited for: 2 -> 0; matrix products, arithmetic and copies ran while one was open for 0% -> 0% of each run, Pallas kernels for 0% -> 0%
where the time goes in v2:
time: 273 us; the launch traced here: 271 us
  Pallas kernels  240 us (88%)
  matrix products  20.6 us (8%)
  local copies, waits for them, and re-layouts  10.3 us (4%)
    pallas_call x1, Pallas kernels, gather(): pl.pallas_call(functools.partial(gather_kernel, (rows, chips, orb_local,...  145 us
    pallas_call x1, Pallas kernels, finish(): pl.pallas_call(functools.partial(finish_kernel, rows, orbs), out_shape=ja...  55.5 us
    pallas_call x1, Pallas kernels, exchange(): pl.pallas_call(functools.partial(exchange_kernel, rows, chips), out_shape...  39.7 us
    dot_general x4, matrix products, per_device(): jnp.einsum('pmk,jk->pjm', slabs[:, b], kept[:, b * kept_width:(b + 1) * k...  12.7 us

profile of v2, /device:TPU:1, one launch (start us, length us, event | category | flops | bytes accessed | tf_op | source)
XLA Modules:
  0.0 271.1 jit_solution(8127295724597329929)
XLA Ops:
  0.0 0.8 reshape.24
  0.8 0.5 pad.4.ids_ref
  1.3 144.7 %shard_map.46 = (bf16[512,10240]{1,0:T(8,128)(2,1)}, bf16[3,256,5120]{2,1,0:T(8,128)(2,1)}) custom-call(s32[1,128]{1,0:T(1,128)} %pad.4.ids_ref, bf16[128,16384]{1,0:T(8,128)(2,1)} %coef_ref.1, bf16[3,256,5120]{2,1,0:T(8,128)(2,1)} %ints_ref.1), custom_call_target="tpu_custom_call" | custom-call | tf_op jit(solution)/shard_map/pallas_call | solution.py:235
  146.0 0.0 slice-start
  146.0 6.0 %fusion.28 = bf16[3,512,128]{1,2,0:T(8,128)(2,1)S(1)} fusion(bf16[3,2,128,5120]{3,2,1,0:T(8,128)(2,1)} %bitcast.111, bf16[512,10240]{1,0:T(8,128)(2,1)} %get-tuple-element.7), kind=kOutput, calls=%fused_computation.27 | convolution fusion | flops 2013462528 | bytes 9568256 | tf_op jit(solution)/shard_map/pmk,jk->pjm/dot_general | solution.py:391
  152.1 0.6 copy-done.1
  152.6 2.2 copy-done.2
  154.9 2.2 fusion.34
  157.1 0.2 slice-done.1
  157.4 2.2 fusion.31
  159.6 2.2 fusion.37
  161.8 0.1 maximum_maximum_fusion
  161.9 0.9 copy.11
  162.8 0.0 copy-start
  162.8 1.3 copy.29
  164.1 39.7 %shard_map.47 = bf16[16,6,32,256]{3,2,1,0:T(8,128)(2,1)} custom-call(bf16[16,6,32,256]{3,2,1,0:T(8,128)(2,1)} %bitcast.106), custom_call_target="tpu_custom_call" | custom-call | tf_op jit(solution)/shard_map/pallas_call | solution.py:281
  203.9 0.2 reshape.29
  204.0 0.2 rev.3
  204.3 0.2 reshape.34
  204.4 3.3 %fusion.14 = bf16[4,32,256,24]{2,3,1,0:T(8,128)(2,1)S(1)} fusion(bf16[4,24,32,256]{3,2,1,0:T(8,128)(2,1)} %bitcast.103, f32[24,24,1,1]{1,0,2,3:T(8,128)S(1)} %reshape.34), kind=kOutput, calls=%fused_computation.20 | convolution fusion | flops 226492416 | bytes 3148032 | tf_op jit(solution)/shard_map/pq,rpjm->rqjm/dot_general | solution.py:407
  207.7 4.6 %bitcast_convert_fusion = bf16[4,256,4,256]{1,3,2,0:T(8,128)(2,1)} fusion(bf16[4,24,32,256,1]{3,2,1,0,4:T(8,128)(2,1)} %bitcast.104, bf16[4,32,256,24]{2,3,1,0:T(8,128)(2,1)S(1)} %fusion.14), kind=kOutput, calls=%fused_computation.12 | convolution fusion | flops 1611661312 | bytes 5242880 | tf_op jit(solution)/shard_map/rqjm,sqjn->srmn/dot_general | solution.py:410
  212.4 1.7 slice.29.coef_ref
  214.0 55.5 %shard_map.48 = f32[128,256]{1,0:T(8,128)} custom-call(bf16[4,1024,256]{2,1,0:T(8,128)(2,1)} %bitcast.107, bf16[128,1024]{1,0:T(8,128)(2,1)} %slice.29.coef_ref), custom_call_target="tpu_custom_call" | custom-call | tf_op jit(solution)/shard_map/pallas_call | solution.py:349
  269.6 1.6 copy.31
  (7 shorter events, 0.0 us)
Async XLA Ops:
  146.0 6.7 %copy-start.1 = (bf16[512,10240]{1,0:T(8,128)(2,1)S(1)}, bf16[512,10240]{1,0:T(8,128)(2,1)}, u32[]{:S(2)}) copy-start(bf16[512,10240]{1,0:T(8,128)(2,1)} %get-tuple-element.7) | copy-start | bytes 31457284
  146.0 8.9 %copy-start.2 = (bf16[3,256,5120]{2,1,0:T(8,128)(2,1)S(1)}, bf16[3,256,5120]{2,1,0:T(8,128)(2,1)}, u32[]{:S(2)}) copy-start(bf16[3,256,5120]{2,1,0:T(8,128)(2,1)} %get-tuple-element.8) | copy-start | bytes 23592964
  146.0 11.1 %slice-start = ((s8[7864320]{0:T(1024)(128)(4,1)}), s8[4194304]{0:T(1024)(128)(4,1)S(1)}, s32[]{:S(2)}) async-start(s8[7864320]{0:T(1024)(128)(4,1)} %bitcast.99), calls=%async_computation | async-start | bytes 8388608
  154.9 2.5 slice-start.1
  162.8 41.0 %copy-start = (f32[24,24]{1,0:T(8,128)S(1)}, f32[24,24]{1,0:T(8,128)}, u32[]{:S(2)}) copy-start(f32[24,24]{1,0:T(8,128)} %param.7) | copy-start | bytes 6916

commit v3 on v2

--- a/solution.py
+++ b/solution.py
@@ -84,7 +84,7 @@
     def z_copy(route, h, device):
         rows_at = pl.ds(pl.multiple_of(row * quarter + h * piece, piece), piece)
         return remote(
-            own.at[:, rows_at, :],
+            own.at[:, rows_at, :] if routes[route][0] == 1 else raw[route - 2, h],
             raw[route, h],
             z_send.at[route, h],
             z_recv.at[route, h],
@@ -93,8 +93,9 @@
 
     def towards(route):
         d, s = routes[route]
-        there = chip + s * d
-        return there, (there >= 0) & (there < chips)
+        there = chip + s
+        start = chip - s * (d - 1)
+        return there, (there >= 0) & (there < chips) & (start >= 0) & (start < chips)
 
     def origin(route):
         d, s = routes[route]
@@ -122,7 +123,7 @@
         return carry
 
     lax.fori_loop(0, tiles, landed, 0)
-    for route in range(len(routes)):
+    for route in range(2):
         there, valid = towards(route)
         for h in range(SPLIT):
 
@@ -184,6 +185,13 @@
                 @pl.when(valid)
                 def _():
                     z_copy(route, h, partner).wait_recv()
+                    if d + 1 < chips:
+                        there, onward = towards(route + 2)
+
+                        @pl.when(onward)
+                        def _():
+                            z_copy(route + 2, h, (row, there * CORES + core)).start()
+
                     for t in range(1, rows):
                         take(raw[route, h], staged[route, h, t], t)
                         spread(route, h, t, row, came, row_peers[rows - t - 1]).start()
@@ -292,77 +300,133 @@
     )(outgoing)
 
 
-def finish_kernel(rows, orbs, gram_ref, coef_ref, out_ref, *scratch):
-    (part1, sum1, part2, share, full, send1, recv1, send2, recv2, send3, recv3) = scratch
+def finish_kernel(rows, chips, gram_ref, coef_ref, out_ref, *scratch):
+    part0, sum0, part1, sum1, part2, share, full = scratch[:7]
+    send0, recv0, send1, recv1, send2, recv2, send3, recv3 = scratch[7:]
     row = lax.axis_index("row")
     orb = lax.axis_index("orb")
+    chip = orb // CORES
+    core = orb % CORES
     height = share.shape[0]
+    half = height * chips
+    partner = (row, chip * CORES + 1 - core)
     row_peers = [lax.rem(row + t, rows) for t in range(1, rows)]
-    orb_peers = [lax.rem(orb + t, orbs) for t in range(1, orbs)]
-    greet([(peer, orb) for peer in row_peers] + [(row, peer) for peer in orb_peers])
-    copies = []
-    for t, peer in enumerate(row_peers):
-        copies.append(
-            remote(gram_ref.at[peer], part1.at[t], send1.at[t], recv1.at[t], (peer, orb))
-        )
-        copies[-1].start()
-    for copy in copies:
-        copy.wait()
-    total = gram_ref[row].astype(jnp.float32)
+    chip_peers = [lax.rem(chip + t, chips) for t in range(1, chips)]
+    greet(
+        [partner]
+        + [(peer, orb) for peer in row_peers]
+        + [(row, peer * CORES + core) for peer in chip_peers]
+    )
+    order = row_peers + [row]
+    first = []
+    for t, peer in enumerate(order):
+        first.append(
+            remote(
+                gram_ref.at[peer, 1 - core], part0.at[peer], send0.at[t], recv0.at[t], partner
+            )
+        )
+        first[-1].start()
+    second = []
+    for t, peer in enumerate(order):
+        first[t].wait_recv()
+        total = gram_ref[peer, core].astype(jnp.float32) + part0[peer].astype(jnp.float32)
+        sum0[peer] = total.astype(sum0.dtype)
+        if t < rows - 1:
+            second.append(
+                remote(sum0.at[peer], part1.at[t], send1.at[t], recv1.at[t], (peer, orb))
+            )
+            second[-1].start()
+    for copy in second:
+        copy.wait_recv()
+    total = sum0[row].astype(jnp.float32)
     for t in range(rows - 1):
         total = total + part1[t].astype(jnp.float32)
     sum1[...] = total.astype(sum1.dtype).reshape(sum1.shape)
-    copies = []
-    for t, peer in enumerate(orb_peers):
-        copies.append(
-            remote(sum1.at[peer], part2.at[t], send2.at[t], recv2.at[t], (row, peer))
-        )
-        copies[-1].start()
-    for copy in copies:
-        copy.wait()
-    total = sum1[orb].astype(jnp.float32)
-    for t in range(orbs - 1):
+    third = []
+    for t, peer in enumerate(chip_peers):
+        device = (row, peer * CORES + core)
+        third.append(remote(sum1.at[peer], part2.at[t], send2.at[t], recv2.at[t], device))
+        third[-1].start()
+    for copy in third:
+        copy.wait_recv()
+    total = sum1[chip].astype(jnp.float32)
+    for t in range(chips - 1):
         total = total + part2[t].astype(jnp.float32)
     share[...] = total.astype(share.dtype)
-    own_rows = pl.ds(pl.multiple_of(orb * height, height), height)
-    copies = []
-    for t, peer in enumerate(orb_peers):
-        copies.append(
-            remote(share, full.at[own_rows, :], send3.at[t], recv3.at[t], (row, peer))
-        )
-        copies[-1].start()
-    full[own_rows, :] = share[...]
-    for t in range(orbs - 1):
-        copies[t].wait_send()
-        source = lax.rem(orb + orbs - t - 1, orbs)
-        rows_at = pl.ds(pl.multiple_of(source * height, height), height)
+
+    def block(from_core, from_chip):
+        start = pl.multiple_of(from_core * half + from_chip * height, height)
+        return full.at[pl.ds(start, height), :]
+
+    fourth = [
+        remote(share, block(core, chip), send3.at[0, 0], recv3.at[0, 0], partner)
+    ]
+    for t, peer in enumerate(chip_peers):
+        device = (row, peer * CORES + core)
+        fourth.append(
+            remote(share, block(core, chip), send3.at[0, t + 1], recv3.at[0, t + 1], device)
+        )
+    for copy in fourth:
+        copy.start()
+    full[pl.ds(pl.multiple_of(core * half + chip * height, height), height), :] = share[...]
+    passed = []
+    for t in range(1, chips):
+        source = lax.rem(chip + chips - t, chips)
         remote(
-            share, full.at[rows_at, :], send3.at[t], recv3.at[t], (row, orb_peers[0])
+            share, block(core, source), send3.at[0, t], recv3.at[0, t], partner
         ).wait_recv()
-    out_ref[...] = jnp.dot(coef_ref[...], full[...], preferred_element_type=jnp.float32)
-
-
-def finish(gram, coefs, rows, orbs):
-    _, window, width = gram.shape
-    height = window // orbs
+        passed.append(
+            remote(
+                block(core, source),
+                block(core, source),
+                send3.at[1, t],
+                recv3.at[1, t],
+                partner,
+            )
+        )
+        passed[-1].start()
+    mine = pl.ds(pl.multiple_of(core * half, half), half)
+    theirs = pl.ds(pl.multiple_of((1 - core) * half, half), half)
+    result = jnp.dot(coef_ref[:, mine], full[mine, :], preferred_element_type=jnp.float32)
+    remote(share, block(1 - core, chip), send3.at[0, 0], recv3.at[0, 0], partner).wait_recv()
+    for t in range(1, chips):
+        source = lax.rem(chip + chips - t, chips)
+        remote(
+            block(core, source), block(1 - core, source), send3.at[1, t], recv3.at[1, t], partner
+        ).wait_recv()
+    out_ref[...] = result + jnp.dot(
+        coef_ref[:, theirs], full[theirs, :], preferred_element_type=jnp.float32
+    )
+    for copy in first + second + third + fourth + passed:
+        copy.wait_send()
+
+
+def finish(gram, coefs, rows, chips):
+    width = gram.shape[-1]
+    half = gram.shape[2]
+    height = half // chips
     dtype = gram.dtype
     return pl.pallas_call(
-        functools.partial(finish_kernel, rows, orbs),
+        functools.partial(finish_kernel, rows, chips),
         out_shape=jax.ShapeDtypeStruct((coefs.shape[0], width), jnp.float32),
         in_specs=[pl.BlockSpec(memory_space=pltpu.VMEM)] * 2,
         out_specs=pl.BlockSpec(memory_space=pltpu.VMEM),
         scratch_shapes=[
-            pltpu.VMEM((rows - 1, window, width), dtype),
-            pltpu.VMEM((orbs, height, width), dtype),
-            pltpu.VMEM((orbs - 1, height, width), dtype),
+            pltpu.VMEM((rows, half, width), dtype),
+            pltpu.VMEM((rows, half, width), dtype),
+            pltpu.VMEM((rows - 1, half, width), dtype),
+            pltpu.VMEM((chips, height, width), dtype),
+            pltpu.VMEM((chips - 1, height, width), dtype),
             pltpu.VMEM((height, width), dtype),
-            pltpu.VMEM((window, width), dtype),
+            pltpu.VMEM((CORES * half, width), dtype),
             pltpu.SemaphoreType.DMA((rows,)),
             pltpu.SemaphoreType.DMA((rows,)),
-            pltpu.SemaphoreType.DMA((orbs,)),
-            pltpu.SemaphoreType.DMA((orbs,)),
-            pltpu.SemaphoreType.DMA((orbs,)),
-            pltpu.SemaphoreType.DMA((orbs,)),
+            pltpu.SemaphoreType.DMA((rows,)),
+            pltpu.SemaphoreType.DMA((rows,)),
+            pltpu.SemaphoreType.DMA((chips,)),
+            pltpu.SemaphoreType.DMA((chips,)),
+            pltpu.SemaphoreType.DMA((CORES, chips)),
+            pltpu.SemaphoreType.DMA((CORES, chips)),
         ],
         compiler_params=pltpu.CompilerParams(collective_id=2, has_side_effects=True),
     )(gram, coefs)
@@ -410,8 +474,8 @@
     gram = jnp.einsum(
         "rqjm,sqjn->srmn", by_part, mixed, preferred_element_type=jnp.float32
     ).astype(jnp.bfloat16)
-    gram = gram.reshape(rows, window, local_rows)
-    return finish(gram, coefficients[:, :window], rows, orbs)
+    gram = gram.reshape(rows, CORES, window // CORES, local_rows)
+    return finish(gram, coefficients[:, :window], rows, chips)
 
 
 def plain_device(rows, orbs, integrals, tile_ids, coefficients, metric):

time: 273 us -> 213 us (0.78)
  Pallas kernels: 240 us -> 181 us
    pallas_call x1, Pallas kernels: 145 us -> 105 us  [gather(): pl.pallas_call(functools.partial(gather_kernel, (rows, chips, orb_local,...]
    pallas_call x1, Pallas kernels: 55.5 us -> 36.3 us  [finish(): pl.pallas_call(functools.partial(finish_kernel, rows, chips), out_shape=j...]
where the time goes in v3:
time: 213 us
  Pallas kernels  181 us (85%)
  matrix products  20.6 us (10%)
  local copies, waits for them, and re-layouts  10.3 us (5%)
    pallas_call x1, Pallas kernels, gather(): pl.pallas_call(functools.partial(gather_kernel, (rows, chips, orb_local,...  105 us
    pallas_call x1, Pallas kernels, exchange(): pl.pallas_call(functools.partial(exchange_kernel, rows, chips), out_shape...  39.7 us
    pallas_call x1, Pallas kernels, finish(): pl.pallas_call(functools.partial(finish_kernel, rows, chips), out_shape=j...  36.3 us
    dot_general x4, matrix products, per_device(): jnp.einsum('pmk,jk->pjm', slabs[:, b], kept[:, b * kept_width:(b + 1) * k...  12.7 us
    unnamed x11, local copies, waits for them, and re-layouts  4.64 us
    dot_general x1, matrix products, per_device(): jnp.einsum('rqjm,sqjn->srmn', by_part, mixed, preferred_element_type=jnp....  4.62 us

profile of v3, /device:TPU:1, one launch (start us, length us, event | category | flops | bytes accessed | tf_op | source)
XLA Modules:
  0.0 212.6 jit_solution(10486883540646616307)
XLA Ops:
  0.0 0.8 reshape.24
  0.8 0.5 pad.4.ids_ref
  1.3 105.5 %shard_map.46 = (bf16[512,10240]{1,0:T(8,128)(2,1)}, bf16[3,256,5120]{2,1,0:T(8,128)(2,1)}) custom-call(s32[1,128]{1,0:T(1,128)} %pad.4.ids_ref, bf16[128,16384]{1,0:T(8,128)(2,1)} %coef_ref.1, bf16[3,256,5120]{2,1,0:T(8,128)(2,1)} %ints_ref.1), custom_call_target="tpu_custom_call" | custom-call | tf_op jit(solution)/shard_map/pallas_call | solution.py:243
  106.8 0.0 slice-start
  106.8 6.0 %fusion.28 = bf16[3,512,128]{1,2,0:T(8,128)(2,1)S(1)} fusion(bf16[3,2,128,5120]{3,2,1,0:T(8,128)(2,1)} %bitcast.111, bf16[512,10240]{1,0:T(8,128)(2,1)} %get-tuple-element.7), kind=kOutput, calls=%fused_computation.27 | convolution fusion | flops 2013462528 | bytes 9568256 | tf_op jit(solution)/shard_map/pmk,jk->pjm/dot_general | solution.py:455
  112.8 0.6 copy-done.1
  113.4 2.2 %copy-done.2 = bf16[3,256,5120]{2,1,0:T(8,128)(2,1)S(1)} copy-done((bf16[3,256,5120]{2,1,0:T(8,128)(2,1)S(1)}, bf16[3,256,5120]{2,1,0:T(8,128)(2,1)}, u32[]{:S(2)}) %copy-start.2) | copy-done | bytes 7864344
  115.6 2.2 %fusion.34 = bf16[3,512,128]{1,2,0:T(8,128)(2,1)S(1)} fusion(bf16[3,2,128,5120]{3,2,1,0:T(8,128)(2,1)S(1)} %bitcast.112, bf16[512,10240]{1,0:T(8,128)(2,1)S(1)} %copy-done.1), kind=kOutput, calls=%fused_computation.29 | convolution fusion | flops 2013462528 | bytes 9568256 | tf_op jit(solution)/shard_map/pmk,jk->pjm/dot_general | solution.py:455
  117.9 0.2 slice-done.1
  118.1 2.2 %fusion.31 = bf16[3,512,128]{1,2,0:T(8,128)(2,1)S(1)} fusion(bf16[3,2,128,5120]{3,2,1,0:T(8,128)(2,1)S(1)} %bitcast.101, bf16[512,10240]{1,0:T(8,128)(2,1)S(1)} %copy-done.1), kind=kOutput, calls=%fused_computation.28 | convolution fusion | flops 2013462528 | bytes 9568256 | tf_op jit(solution)/shard_map/pmk,jk->pjm/dot_general | solution.py:455
  120.4 2.2 %fusion.37 = bf16[3,512,128]{1,2,0:T(8,128)(2,1)S(1)} fusion(bf16[3,2,128,5120]{3,2,1,0:T(8,128)(2,1)S(1)} %bitcast.102, bf16[512,10240]{1,0:T(8,128)(2,1)S(1)} %copy-done.1), kind=kOutput, calls=%fused_computation.30 | convolution fusion | flops 2013462528 | bytes 9568256 | tf_op jit(solution)/shard_map/pmk,jk->pjm/dot_general | solution.py:455
  122.6 0.1 maximum_maximum_fusion
  122.7 0.9 copy.11
  123.6 0.0 copy-start
  123.6 1.3 copy.29
  124.9 39.7 %shard_map.47 = bf16[16,6,32,256]{3,2,1,0:T(8,128)(2,1)} custom-call(bf16[16,6,32,256]{3,2,1,0:T(8,128)(2,1)} %bitcast.106), custom_call_target="tpu_custom_call" | custom-call | tf_op jit(solution)/shard_map/pallas_call | solution.py:289
  164.6 0.2 reshape.29
  164.7 0.2 rev.3
  165.0 0.2 reshape.34
  165.2 3.3 %fusion.14 = bf16[4,32,256,24]{2,3,1,0:T(8,128)(2,1)S(1)} fusion(bf16[4,24,32,256]{3,2,1,0:T(8,128)(2,1)} %bitcast.103, f32[24,24,1,1]{1,0,2,3:T(8,128)S(1)} %reshape.34), kind=kOutput, calls=%fused_computation.20 | convolution fusion | flops 226492416 | bytes 3148032 | tf_op jit(solution)/shard_map/pq,rpjm->rqjm/dot_general | solution.py:471
  168.5 4.6 %bitcast_convert_fusion = bf16[4,256,4,256]{1,3,2,0:T(8,128)(2,1)} fusion(bf16[4,24,32,256,1]{3,2,1,0,4:T(8,128)(2,1)} %bitcast.104, bf16[4,32,256,24]{2,3,1,0:T(8,128)(2,1)S(1)} %fusion.14), kind=kOutput, calls=%fused_computation.12 | convolution fusion | flops 1611661312 | bytes 5242880 | tf_op jit(solution)/shard_map/rqjm,sqjn->srmn/dot_general | solution.py:474
  173.1 1.7 slice.29.coef_ref
  174.7 36.3 %shard_map.48 = f32[128,256]{1,0:T(8,128)} custom-call(bf16[4,2,512,256]{3,2,1,0:T(8,128)(2,1)} %bitcast.107, bf16[128,1024]{1,0:T(8,128)(2,1)} %slice.29.coef_ref), custom_call_target="tpu_custom_call" | custom-call | tf_op jit(solution)/shard_map/pallas_call | solution.py:409
  211.1 1.6 copy.31
  (7 shorter events, 0.0 us)
Async XLA Ops:
  106.8 6.7 %copy-start.1 = (bf16[512,10240]{1,0:T(8,128)(2,1)S(1)}, bf16[512,10240]{1,0:T(8,128)(2,1)}, u32[]{:S(2)}) copy-start(bf16[512,10240]{1,0:T(8,128)(2,1)} %get-tuple-element.7) | copy-start | bytes 31457284
  106.8 8.9 %copy-start.2 = (bf16[3,256,5120]{2,1,0:T(8,128)(2,1)S(1)}, bf16[3,256,5120]{2,1,0:T(8,128)(2,1)}, u32[]{:S(2)}) copy-start(bf16[3,256,5120]{2,1,0:T(8,128)(2,1)} %get-tuple-element.8) | copy-start | bytes 23592964
  106.8 11.1 %slice-start = ((s8[7864320]{0:T(1024)(128)(4,1)}), s8[4194304]{0:T(1024)(128)(4,1)S(1)}, s32[]{:S(2)}) async-start(s8[7864320]{0:T(1024)(128)(4,1)} %bitcast.99), calls=%async_computation | async-start | bytes 8388608
  115.6 2.5 %slice-start.1 = ((s8[7864320]{0:T(1024)(128)(4,1)}), s8[3670016]{0:T(1024)(128)(4,1)S(1)}, s32[]{:S(2)}) async-start(s8[7864320]{0:T(1024)(128)(4,1)} %bitcast.99), calls=%async_computation.1 | async-start | bytes 7340032
  123.6 41.0 %copy-start = (f32[24,24]{1,0:T(8,128)S(1)}, f32[24,24]{1,0:T(8,128)}, u32[]{:S(2)}) copy-start(f32[24,24]{1,0:T(8,128)} %param.7) | copy-start | bytes 6916

commit v4 on v3

--- a/solution.py
+++ b/solution.py
@@ -56,8 +56,8 @@
     )
 
 
-def gather_kernel(dims, ids_ref, coef_ref, ints_ref, kept_ref, other_ref, *scratch):
-    rows, chips, orb_local, tile, count = dims
+def halves_kernel(dims, ids_ref, coef_ref, ints_ref, out_ref, *scratch):
+    rows, chips, orb_local, tile, count, aux_local, blocks, part = dims
     quarter = orb_local // rows
     piece = quarter // SPLIT
     routes = [(d, s) for d in range(1, chips) for s in (1, -1)]
@@ -66,20 +66,23 @@
     for route in range(len(routes)):
         for h in range(SPLIT):
             raw[route, h] = scratch.pop(0)
-    staged = {}
-    for route in range(len(routes)):
-        for h in range(SPLIT):
-            for t in range(rows):
-                staged[route, h, t] = scratch.pop(0)
-    own, own_kept, ids_v, ids_s, z_send, z_recv, p_send, p_recv, l_sem, i_send, i_recv = scratch
+    own, kept, staged, both, ready, ids_v, ids_s = scratch[:7]
+    z_send, z_recv, p_send, p_recv, l_sem, i_send, i_recv, x_send, x_recv = scratch[7:]
+    width = count * tile // blocks
+    total = rows * chips
     row = lax.axis_index("row")
     orb = lax.axis_index("orb")
     chip = orb // CORES
     core = orb % CORES
     row_peers = [(lax.rem(row + t, rows), orb) for t in range(1, rows)]
-    chip_peers = [(row, lax.rem(chip + d, chips) * CORES + core) for d in range(1, chips)]
     partner = (row, chip * CORES + 1 - core)
-    greet(row_peers + chip_peers + [partner])
+    me = row * chips + chip
+
+    def place(k):
+        other = lax.rem(me + k, total)
+        return other, (other // chips, lax.rem(other, chips) * CORES + core)
+
+    greet([place(k)[1] for k in range(1, total)] + [partner])
 
     def z_copy(route, h, device):
         rows_at = pl.ds(pl.multiple_of(row * quarter + h * piece, piece), piece)
@@ -131,8 +134,10 @@
             def _():
                 z_copy(route, h, (row, there * CORES + core)).start()
 
-    swap = remote(ints_ref, other_ref, i_send.at[0], i_recv.at[0], partner)
+    swap = remote(ints_ref, both.at[1], i_send.at[0], i_recv.at[0], partner)
     swap.start()
+    bring = pltpu.make_async_copy(ints_ref, both.at[0], l_sem.at[2])
+    bring.start()
     first = pltpu.make_async_copy(ids_ref, ids_s.at[0], l_sem.at[1])
     first.start()
     first.wait()
@@ -154,28 +159,57 @@
 
         lax.fori_loop(0, count // step, some, 0)
 
-    take(own, own_kept, 0)
-    own_rows = pl.ds(pl.multiple_of(chip * orb_local, orb_local), orb_local)
-    keep_own = pltpu.make_async_copy(own_kept, kept_ref.at[own_rows, :], l_sem.at[0])
-    keep_own.start()
-
-    def spread(route, h, t, from_row, from_chip, device):
-        start = pl.multiple_of(from_chip * orb_local + from_row * quarter + h * piece, piece)
+    def band(from_row, h):
+        return pl.ds(pl.multiple_of(from_row * quarter + h * piece, piece), piece)
+
+    def spread(from_row, came, h, t, device):
+        k = lax.rem(came + chips - chip, chips) - 1
         return remote(
-            staged[route, h, t],
-            kept_ref.at[pl.ds(start, piece), :],
-            p_send.at[route, h, t],
-            p_recv.at[route, h, t],
+            staged.at[k, h, t - 1],
+            kept.at[came, band(from_row, h), :],
+            p_send.at[k, h, t],
+            p_recv.at[k, h, t],
             device,
         )
 
-    def local(route, h, from_chip):
-        start = pl.multiple_of(from_chip * orb_local + row * quarter + h * piece, piece)
+    def handout(came, k):
+        other, device = place(k)
+        return remote(
+            ready.at[came, other],
+            out_ref.at[me, :, came],
+            x_send.at[came, k],
+            x_recv.at[came, k],
+            device,
+        )
+
+    def keep(came):
         return pltpu.make_async_copy(
-            staged[route, h, 0], kept_ref.at[pl.ds(start, piece), :], p_send.at[route, h, 0]
-        )
-
-    for d in range(1, chips):
+            ready.at[came, me], out_ref.at[me, :, came], x_send.at[came, 0]
+        )
+
+    def product(came):
+        def one(step, carry):
+            side = step // blocks
+            block = step - side * blocks
+            lhs = kept[came, :, pl.ds(pl.multiple_of(block * width, width), width)]
+            at = pl.ds(pl.multiple_of(block * tile, tile), tile)
+            rhs = both[side, :, at, :].reshape(aux_local * tile, width)
+            result = lax.dot_general(
+                lhs, rhs, (((1,), (1,)), ((), ())), preferred_element_type=jnp.float32
+            )
+            for p in range(aux_local):
+                value = result[:, p * tile : (p + 1) * tile].astype(ready.dtype)
+                ready[came, :, side * aux_local + p, :, at] = value.reshape(total, part, tile)
+            return carry
+
+        lax.fori_loop(0, CORES * blocks, one, 0)
+        for k in range(1, total):
+            handout(came, k).start()
+        keep(came).start()
+
+    take(own, kept.at[chip], 0)
+
+    def pass_on(d):
         for h in range(SPLIT):
             for route in range(len(routes)):
                 if routes[route][0] != d:
@@ -192,11 +226,35 @@
                         def _():
                             z_copy(route + 2, h, (row, there * CORES + core)).start()
 
+                    k = lax.rem(came + chips - chip, chips) - 1
                     for t in range(1, rows):
-                        take(raw[route, h], staged[route, h, t], t)
-                        spread(route, h, t, row, came, row_peers[rows - t - 1]).start()
-                    take(raw[route, h], staged[route, h, 0], 0)
-                    local(route, h, came).start()
+                        take(raw[route, h], staged.at[k, h, t - 1], t)
+                        spread(row, came, h, t, row_peers[rows - t - 1]).start()
+                    take(raw[route, h], kept.at[came, band(row, h), :], 0)
+
+    def multiply(d):
+        for route in range(len(routes)):
+            if routes[route][0] != d:
+                continue
+            came, valid = origin(route)
+
+            @pl.when(valid)
+            def _():
+                for h in range(SPLIT):
+                    for t in range(1, rows):
+                        source_row = lax.rem(row + t, rows)
+                        spread(source_row, came, h, t, row_peers[0]).wait_recv()
+                product(came)
+
+    for d in range(1, chips):
+        pass_on(d)
+        if d == 1:
+            bring.wait()
+            swap.wait()
+            product(chip)
+        else:
+            multiply(d - 1)
+    multiply(chips - 1)
 
     for route in range(len(routes)):
         there, sent = towards(route)
@@ -209,95 +267,68 @@
 
             @pl.when(valid)
             def _():
-                local(route, h, came).wait()
                 for t in range(1, rows):
-                    spread(route, h, t, row, came, row_peers[rows - t - 1]).wait_send()
-                    source_row = lax.rem(row + t, rows)
-                    spread(route, h, t, source_row, came, row_peers[0]).wait_recv()
-
-    keep_own.wait()
-    swap.wait()
-
-
-def gather(integrals, ids, coefficients, rows, orbs, tile, count):
+                    spread(row, came, h, t, row_peers[rows - t - 1]).wait_send()
+
+    for came in range(chips):
+        keep(came).wait()
+        for k in range(1, total):
+            handout(came, k).wait_send()
+            other, device = place(total - k)
+            remote(
+                ready.at[came, me],
+                out_ref.at[other, :, came],
+                x_send.at[came, k],
+                x_recv.at[came, k],
+                device,
+            ).wait_recv()
+
+
+def halves_by_part(integrals, ids, coefficients, rows, orbs, blocks, count):
     chips = orbs // CORES
     orb_local, basis = coefficients.shape
+    aux_local, local_rows, _ = integrals.shape
+    tile = local_rows // blocks
+    total = rows * chips
+    part = orb_local // total
     piece = orb_local // rows // SPLIT
     routes = 2 * (chips - 1)
     dtype = coefficients.dtype
-    scratch = [pltpu.VMEM((basis // tile, piece, tile), dtype) for _ in range(routes * SPLIT)]
-    scratch += [pltpu.VMEM((piece, count * tile), dtype) for _ in range(routes * SPLIT * rows)]
+    scratch = [
+        pltpu.VMEM((basis // tile, piece, tile), dtype) for _ in range(routes * SPLIT)
+    ]
     scratch += [
         pltpu.VMEM((basis // tile, orb_local, tile), dtype),
-        pltpu.VMEM((orb_local, count * tile), dtype),
+        pltpu.VMEM((chips, orb_local, count * tile), dtype),
+        pltpu.VMEM((chips - 1, SPLIT, rows - 1, piece, count * tile), dtype),
+        pltpu.VMEM((CORES,) + integrals.shape, dtype),
+        pltpu.VMEM((chips, total, CORES * aux_local, part, local_rows), dtype),
         pltpu.VMEM((rows, 1, ids.shape[1]), jnp.int32),
         pltpu.SMEM((rows, 1, ids.shape[1]), jnp.int32),
         pltpu.SemaphoreType.DMA((routes, SPLIT)),
         pltpu.SemaphoreType.DMA((routes, SPLIT)),
-        pltpu.SemaphoreType.DMA((routes, SPLIT, rows)),
-        pltpu.SemaphoreType.DMA((routes, SPLIT, rows)),
-        pltpu.SemaphoreType.DMA((2,)),
+        pltpu.SemaphoreType.DMA((chips - 1, SPLIT, rows)),
+        pltpu.SemaphoreType.DMA((chips - 1, SPLIT, rows)),
+        pltpu.SemaphoreType.DMA((3,)),
         pltpu.SemaphoreType.DMA((rows,)),
         pltpu.SemaphoreType.DMA((rows,)),
+        pltpu.SemaphoreType.DMA((chips, total)),
+        pltpu.SemaphoreType.DMA((chips, total)),
     ]
+    dims = (rows, chips, orb_local, tile, count, aux_local, blocks, part)
     return pl.pallas_call(
-        functools.partial(gather_kernel, (rows, chips, orb_local, tile, count)),
-        out_shape=(
-            jax.ShapeDtypeStruct((chips * orb_local, count * tile), dtype),
-            jax.ShapeDtypeStruct(integrals.shape, integrals.dtype),
+        functools.partial(halves_kernel, dims),
+        out_shape=jax.ShapeDtypeStruct(
+            (total, CORES * aux_local, chips, part, local_rows), dtype
         ),
         in_specs=[pl.BlockSpec(memory_space=pltpu.VMEM)]
         + [pl.BlockSpec(memory_space=pl.ANY)] * 2,
-        out_specs=(pl.BlockSpec(memory_space=pl.ANY), pl.BlockSpec(memory_space=pl.ANY)),
+        out_specs=pl.BlockSpec(memory_space=pl.ANY),
         scratch_shapes=scratch,
         compiler_params=pltpu.CompilerParams(
-            collective_id=0, has_side_effects=True, vmem_limit_bytes=56 << 20
+            collective_id=0, has_side_effects=True, vmem_limit_bytes=60 << 20
         ),
     )(ids, coefficients, integrals)
-
-
-def exchange_kernel(rows, chips, in_ref, out_ref, send, recv, l_sem):
-    row = lax.axis_index("row")
-    orb = lax.axis_index("orb")
-    core = orb % CORES
-    me = row * chips + orb // CORES
-    total = rows * chips
-
-    def place(k):
-        other = lax.rem(me + k, total)
-        return other, (other // chips, lax.rem(other, chips) * CORES + core)
-
-    greet([place(k)[1] for k in range(1, total)])
-    stay = pltpu.make_async_copy(in_ref.at[me], out_ref.at[me], l_sem)
-    stay.start()
-    copies = []
-    for k in range(1, total):
-        other, device = place(k)
-        copies.append(
-            remote(in_ref.at[other], out_ref.at[me], send.at[k], recv.at[k], device)
-        )
-        copies[-1].start()
-    stay.wait()
-    for k in range(1, total):
-        copies[k - 1].wait_send()
-        other, device = place(total - k)
-        remote(in_ref.at[me], out_ref.at[other], send.at[k], recv.at[k], device).wait_recv()
-
-
-def exchange(outgoing, rows, chips):
-    total = rows * chips
-    return pl.pallas_call(
-        functools.partial(exchange_kernel, rows, chips),
-        out_shape=jax.ShapeDtypeStruct(outgoing.shape, outgoing.dtype),
-        in_specs=[pl.BlockSpec(memory_space=pltpu.VMEM)],
-        out_specs=pl.BlockSpec(memory_space=pltpu.VMEM),
-        scratch_shapes=[
-            pltpu.SemaphoreType.DMA((total,)),
-            pltpu.SemaphoreType.DMA((total,)),
-            pltpu.SemaphoreType.DMA,
-        ],
-        compiler_params=pltpu.CompilerParams(collective_id=1, has_side_effects=True),
-    )(outgoing)
 
 
 def finish_kernel(rows, chips, gram_ref, coef_ref, out_ref, *scratch):
@@ -436,9 +467,8 @@
     aux_local, local_rows, kept_width = integrals.shape
     orb_local, basis_width = coefficients.shape
     block_count, kept_count = tile_ids.shape
-    if orb_local % (16 * SPLIT * rows) or orbs % CORES or (block_count * kept_count) % 8:
+    if orb_local % (16 * SPLIT * rows) or orb_local * CORES % (8 * rows * orbs) or block_count * kept_count % 8:
         return plain_device(rows, orbs, integrals, tile_ids, coefficients, metric)
-    tile_rows = local_rows // block_count
     chips = orbs // CORES
     aux = aux_local * orbs
     window = local_rows * rows
@@ -447,23 +477,7 @@
     part = held // (rows * chips)
     lanes = -(-count // 128) * 128
     ids = jnp.pad(tile_ids.reshape(1, count), ((0, 0), (0, lanes - count)))
-    kept, other = gather(integrals, ids, coefficients, rows, orbs, tile_rows, count)
-    halves = []
-    for source in (integrals, other):
-        slabs = source.reshape(aux_local, block_count, tile_rows, kept_width)
-        blocks = [
-            jnp.einsum(
-                "pmk,jk->pjm",
-                slabs[:, b],
-                kept[:, b * kept_width : (b + 1) * kept_width],
-                preferred_element_type=jnp.float32,
-            ).astype(jnp.bfloat16)
-            for b in range(block_count)
-        ]
-        halves.append(jnp.concatenate(blocks, axis=2))
-    halves = jnp.concatenate(halves, axis=0)
-    outgoing = halves.reshape(CORES * aux_local, rows * chips, part, local_rows)
-    by_part = exchange(outgoing.transpose(1, 0, 2, 3), rows, chips)
+    by_part = halves_by_part(integrals, ids, coefficients, rows, orbs, block_count, count)
     by_part = by_part.reshape(rows, aux, part, local_rows)
     core = lax.axis_index("orb") % CORES
     order = metric.reshape(chips, CORES, aux_local, chips, CORES, aux_local)

time: 213 us -> 182 us (0.85)
  matrix products: 20.6 us -> 6.64 us
  Pallas kernels: 181 us -> 169 us
  local copies, waits for them, and re-layouts: 10.3 us -> 5.81 us
    pallas_call x2 -> x1, Pallas kernels: 145 us -> 129 us  [halves_by_part(): pl.pallas_call(functools.partial(halves_kernel, dims), out_shape=jax.Shap...]
    dot_general x4 -> x0, matrix products: 12.7 us -> none  [per_device(): jnp.einsum('pmk,jk->pjm', slabs[:, b], kept[:, b * kept_width:(b + 1) * k...]
    unnamed x11 -> x3, local copies, waits for them, and re-layouts: 4.64 us -> 1.57 us
    pallas_call x1, Pallas kernels: 36.3 us -> 39.3 us  [finish(): pl.pallas_call(functools.partial(finish_kernel, rows, chips), out_shape=j...]
where the time goes in v4:
time: 182 us; the launch traced here: 181 us
  Pallas kernels  169 us (93%)
  matrix products  6.64 us (4%)
  local copies, waits for them, and re-layouts  5.81 us (3%)
    pallas_call x1, Pallas kernels, halves_by_part(): pl.pallas_call(functools.partial(halves_kernel, dims), out_shape=jax.Shap...  129 us
    pallas_call x1, Pallas kernels, finish(): pl.pallas_call(functools.partial(finish_kernel, rows, chips), out_shape=j...  39.3 us

profile of v4, /device:TPU:1, one launch (start us, length us, event | category | flops | bytes accessed | tf_op | source)
XLA Modules:
  0.0 181.3 jit_solution(3004347969778315624)
XLA Ops:
  0.0 0.9 reshape.17
  0.9 0.2 rev.3
  1.1 0.2 reshape.20
  1.3 0.8 reshape.15
  2.1 0.5 pad.4.ids_ref
  2.6 129.5 %shard_map.46 = bf16[16,6,4,8,256]{4,3,2,1,0:T(8,128)(2,1)} custom-call(s32[1,128]{1,0:T(1,128)} %pad.4.ids_ref, bf16[128,16384]{1,0:T(8,128)(2,1)} %coef_ref.1, bf16[3,256,5120]{2,1,0:T(8,128)(2,1)} %ints_ref.1), custom_call_target="tpu_custom_call" | custom-call | tf_op jit(solution)/shard_map/pallas_call | solution.py:319
  132.1 0.0 copy-start
  132.1 3.4 %fusion.2 = bf16[4,32,256,24]{2,3,1,0:T(8,128)(2,1)S(1)} fusion(bf16[4,24,32,256]{3,2,1,0:T(8,128)(2,1)} %bitcast.23, f32[24,24,1,1]{1,0,2,3:T(8,128)S(1)} %reshape.20), kind=kOutput, calls=%fused_computation.3 | convolution fusion | flops 226492416 | bytes 3148032 | tf_op jit(solution)/shard_map/pq,rpjm->rqjm/dot_general | solution.py:485
  135.5 0.0 copy-done
  135.5 3.2 %bitcast_convert_fusion = bf16[4,256,4,256]{1,3,2,0:T(8,128)(2,1)} fusion(bf16[4,24,32,256,1]{3,2,1,0,4:T(8,128)(2,1)S(1)} %bitcast.24, bf16[4,32,256,24]{2,3,1,0:T(8,128)(2,1)S(1)} %fusion.2), kind=kOutput, calls=%fused_computation | convolution fusion | flops 1611661312 | bytes 5242880 | tf_op jit(solution)/shard_map/rqjm,sqjn->srmn/dot_general | solution.py:488
  138.7 1.7 slice.3.coef_ref
  140.4 39.3 %shard_map.47 = f32[128,256]{1,0:T(8,128)} custom-call(bf16[4,2,512,256]{3,2,1,0:T(8,128)(2,1)} %bitcast.25, bf16[128,1024]{1,0:T(8,128)(2,1)} %slice.3.coef_ref), custom_call_target="tpu_custom_call" | custom-call | tf_op jit(solution)/shard_map/pallas_call | solution.py:440
  179.7 1.6 copy.17
  (1 shorter events, 0.0 us)
Async XLA Ops:
  132.1 3.4 %copy-start = (bf16[16,6,4,8,256]{4,3,2,1,0:T(8,128)(2,1)S(1)}, bf16[16,6,4,8,256]{4,3,2,1,0:T(8,128)(2,1)}, u32[]{:S(2)}) copy-start(bf16[16,6,4,8,256]{4,3,2,1,0:T(8,128)(2,1)} %shard_map.46) | copy-start | bytes 4718596

commit v5 on v4

--- a/solution.py
+++ b/solution.py
@@ -66,8 +66,8 @@
     for route in range(len(routes)):
         for h in range(SPLIT):
             raw[route, h] = scratch.pop(0)
-    own, kept, staged, both, ready, ids_v, ids_s = scratch[:7]
-    z_send, z_recv, p_send, p_recv, l_sem, i_send, i_recv, x_send, x_recv = scratch[7:]
+    own, first_rows, kept, staged, both, ready, ids_v, ids_s = scratch[:8]
+    z_send, z_recv, p_send, p_recv, l_sem, i_send, i_recv, x_send, x_recv = scratch[8:]
     width = count * tile // blocks
     total = rows * chips
     row = lax.axis_index("row")
@@ -85,9 +85,8 @@
     greet([place(k)[1] for k in range(1, total)] + [partner])
 
     def z_copy(route, h, device):
-        rows_at = pl.ds(pl.multiple_of(row * quarter + h * piece, piece), piece)
         return remote(
-            own.at[:, rows_at, :] if routes[route][0] == 1 else raw[route - 2, h],
+            first_rows.at[:, pl.ds(h * piece, piece), :] if routes[route][0] == 1 else raw[route - 2, h],
             raw[route, h],
             z_send.at[route, h],
             z_recv.at[route, h],
@@ -107,12 +106,20 @@
 
     tiles = own.shape[0]
 
-    def fetch(index, carry):
+    def tile_copy(index, source_rows, target, sem):
         at = pl.ds(pl.multiple_of(index * tile, tile), tile)
-        pltpu.make_async_copy(coef_ref.at[:, at], own.at[index], l_sem.at[0]).start()
-        return carry
-
-    lax.fori_loop(0, tiles, fetch, 0)
+        return pltpu.make_async_copy(coef_ref.at[source_rows, at], target.at[index], sem)
+
+    def every(source_rows, target, sem, act):
+        def some(index, carry):
+            act(tile_copy(index, source_rows, target, sem))
+            return carry
+
+        lax.fori_loop(0, tiles, some, 0)
+
+    quarter_rows = pl.ds(pl.multiple_of(row * quarter, quarter), quarter)
+    all_rows = pl.ds(0, orb_local)
+    every(quarter_rows, first_rows, l_sem.at[3], lambda copy: copy.start())
     id_copies = []
     for t in range(1, rows):
         id_copies.append(
@@ -120,12 +127,7 @@
         )
         id_copies[-1].start()
 
-    def landed(index, carry):
-        at = pl.ds(pl.multiple_of(index * tile, tile), tile)
-        pltpu.make_async_copy(coef_ref.at[:, at], own.at[index], l_sem.at[0]).wait()
-        return carry
-
-    lax.fori_loop(0, tiles, landed, 0)
+    every(quarter_rows, first_rows, l_sem.at[3], lambda copy: copy.wait())
     for route in range(2):
         there, valid = towards(route)
         for h in range(SPLIT):
@@ -134,6 +136,7 @@
             def _():
                 z_copy(route, h, (row, there * CORES + core)).start()
 
+    every(all_rows, own, l_sem.at[0], lambda copy: copy.start())
     swap = remote(ints_ref, both.at[1], i_send.at[0], i_recv.at[0], partner)
     swap.start()
     bring = pltpu.make_async_copy(ints_ref, both.at[0], l_sem.at[2])
@@ -207,6 +210,7 @@
             handout(came, k).start()
         keep(came).start()
 
+    every(all_rows, own, l_sem.at[0], lambda copy: copy.wait())
     take(own, kept.at[chip], 0)
 
     def pass_on(d):
@@ -299,6 +303,7 @@
     ]
     scratch += [
         pltpu.VMEM((basis // tile, orb_local, tile), dtype),
+        pltpu.VMEM((basis // tile, orb_local // rows, tile), dtype),
         pltpu.VMEM((chips, orb_local, count * tile), dtype),
         pltpu.VMEM((chips - 1, SPLIT, rows - 1, piece, count * tile), dtype),
         pltpu.VMEM((CORES,) + integrals.shape, dtype),
@@ -309,7 +314,7 @@
         pltpu.SemaphoreType.DMA((routes, SPLIT)),
         pltpu.SemaphoreType.DMA((chips - 1, SPLIT, rows)),
         pltpu.SemaphoreType.DMA((chips - 1, SPLIT, rows)),
-        pltpu.SemaphoreType.DMA((3,)),
+        pltpu.SemaphoreType.DMA((4,)),
         pltpu.SemaphoreType.DMA((rows,)),
         pltpu.SemaphoreType.DMA((rows,)),
         pltpu.SemaphoreType.DMA((chips, total)),
@@ -331,9 +336,13 @@
     )(ids, coefficients, integrals)
 
 
-def finish_kernel(rows, chips, gram_ref, coef_ref, out_ref, *scratch):
-    part0, sum0, part1, sum1, part2, share, full = scratch[:7]
-    send0, recv0, send1, recv1, send2, recv2, send3, recv3 = scratch[7:]
+def finish_kernel(rows, chips, gram_ref, all_ref, out_ref, *scratch):
+    part0, sum0, part1, sum1, part2, share, full, coef_ref = scratch[:8]
+    send0, recv0, send1, recv1, send2, recv2, send3, recv3, l_sem = scratch[8:]
+    window = pltpu.make_async_copy(
+        all_ref.at[:, pl.ds(0, coef_ref.shape[1])], coef_ref, l_sem
+    )
+    window.start()
     row = lax.axis_index("row")
     orb = lax.axis_index("orb")
     chip = orb // CORES
@@ -418,6 +427,7 @@
         passed[-1].start()
     mine = pl.ds(pl.multiple_of(core * half, half), half)
     theirs = pl.ds(pl.multiple_of((1 - core) * half, half), half)
+    window.wait()
     result = jnp.dot(coef_ref[:, mine], full[mine, :], preferred_element_type=jnp.float32)
     remote(share, block(1 - core, chip), send3.at[0, 0], recv3.at[0, 0], partner).wait_recv()
     for t in range(1, chips):
@@ -440,7 +450,10 @@
     return pl.pallas_call(
         functools.partial(finish_kernel, rows, chips),
         out_shape=jax.ShapeDtypeStruct((coefs.shape[0], width), jnp.float32),
-        in_specs=[pl.BlockSpec(memory_space=pltpu.VMEM)] * 2,
+        in_specs=[
+            pl.BlockSpec(memory_space=pltpu.VMEM),
+            pl.BlockSpec(memory_space=pl.ANY),
+        ],
         out_specs=pl.BlockSpec(memory_space=pltpu.VMEM),
         scratch_shapes=[
             pltpu.VMEM((rows, half, width), dtype),
@@ -450,6 +463,7 @@
             pltpu.VMEM((chips - 1, height, width), dtype),
             pltpu.VMEM((height, width), dtype),
             pltpu.VMEM((CORES * half, width), dtype),
+            pltpu.VMEM((coefs.shape[0], CORES * half), dtype),
             pltpu.SemaphoreType.DMA((rows,)),
             pltpu.SemaphoreType.DMA((rows,)),
             pltpu.SemaphoreType.DMA((rows,)),
@@ -458,6 +472,7 @@
             pltpu.SemaphoreType.DMA((chips,)),
             pltpu.SemaphoreType.DMA((CORES, chips)),
             pltpu.SemaphoreType.DMA((CORES, chips)),
+            pltpu.SemaphoreType.DMA,
         ],
         compiler_params=pltpu.CompilerParams(collective_id=2, has_side_effects=True),
     )(gram, coefs)
@@ -489,7 +504,7 @@
         "rqjm,sqjn->srmn", by_part, mixed, preferred_element_type=jnp.float32
     ).astype(jnp.bfloat16)
     gram = gram.reshape(rows, CORES, window // CORES, local_rows)
-    return finish(gram, coefficients[:, :window], rows, chips)
+    return finish(gram, coefficients, rows, chips)
 
 
 def plain_device(rows, orbs, integrals, tile_ids, coefficients, metric):

time: 182 us -> 180 us (0.989)
  no operation moved by 1% of the time
where the time goes in v5:
time: 180 us; the launch traced here: 179 us
  Pallas kernels  168 us (93%)
  matrix products  6.64 us (4%)
  local copies, waits for them, and re-layouts  4.09 us (2%)
    pallas_call x1, Pallas kernels, halves_by_part(): pl.pallas_call(functools.partial(halves_kernel, dims), out_shape=jax.Shap...  129 us
    pallas_call x1, Pallas kernels, finish(): pl.pallas_call(functools.partial(finish_kernel, rows, chips), out_shape=j...  39.3 us

profile of v5, /device:TPU:1, one launch (start us, length us, event | category | flops | bytes accessed | tf_op | source)
XLA Modules:
  0.0 179.2 jit_solution(5091482493730501172)
XLA Ops:
  0.0 0.8 reshape.15
  0.8 0.5 pad.4.ids_ref
  1.3 0.9 reshape.17
  2.2 0.2 rev.3
  2.4 0.2 reshape.20
  2.6 129.1 %shard_map.46 = bf16[16,6,4,8,256]{4,3,2,1,0:T(8,128)(2,1)} custom-call(s32[1,128]{1,0:T(1,128)} %pad.4.ids_ref, bf16[128,16384]{1,0:T(8,128)(2,1)} %all_ref.1, bf16[3,256,5120]{2,1,0:T(8,128)(2,1)} %ints_ref.1), custom_call_target="tpu_custom_call" | custom-call | tf_op jit(solution)/shard_map/pallas_call | solution.py:324
  131.6 0.0 copy-start
  131.6 3.4 %fusion.2 = bf16[4,32,256,24]{2,3,1,0:T(8,128)(2,1)S(1)} fusion(bf16[4,24,32,256]{3,2,1,0:T(8,128)(2,1)} %bitcast.23, f32[24,24,1,1]{1,0,2,3:T(8,128)S(1)} %reshape.20), kind=kOutput, calls=%fused_computation.3 | convolution fusion | flops 226492416 | bytes 3148032 | tf_op jit(solution)/shard_map/pq,rpjm->rqjm/dot_general | solution.py:500
  135.1 0.0 copy-done
  135.1 3.2 %bitcast_convert_fusion = bf16[4,256,4,256]{1,3,2,0:T(8,128)(2,1)} fusion(bf16[4,24,32,256,1]{3,2,1,0,4:T(8,128)(2,1)S(1)} %bitcast.24, bf16[4,32,256,24]{2,3,1,0:T(8,128)(2,1)S(1)} %fusion.2), kind=kOutput, calls=%fused_computation | convolution fusion | flops 1611661312 | bytes 5242880 | tf_op jit(solution)/shard_map/rqjm,sqjn->srmn/dot_general | solution.py:503
  138.3 39.3 %shard_map.47 = f32[128,256]{1,0:T(8,128)} custom-call(bf16[4,2,512,256]{3,2,1,0:T(8,128)(2,1)} %bitcast.25, bf16[128,16384]{1,0:T(8,128)(2,1)} %all_ref.1), custom_call_target="tpu_custom_call" | custom-call | tf_op jit(solution)/shard_map/pallas_call | solution.py:450
  177.6 1.6 copy.17
  (1 shorter events, 0.0 us)
Async XLA Ops:
  131.6 3.4 %copy-start = (bf16[16,6,4,8,256]{4,3,2,1,0:T(8,128)(2,1)S(1)}, bf16[16,6,4,8,256]{4,3,2,1,0:T(8,128)(2,1)}, u32[]{:S(2)}) copy-start(bf16[16,6,4,8,256]{4,3,2,1,0:T(8,128)(2,1)} %shard_map.46) | copy-start | bytes 4718596
